TPU v7x, 32 devices: a whole 2x2x4 slice. The times are simulated.
32 devices in a mesh: ctx: 8 (over z, x), exp: 4 (over y, core).
Axes of the slice: x: 2, y: 2, z: 4, core: 2. Of those that a mesh axis runs over, the one named last changes fastest.
Arguments:
- hidden_states: bfloat16 [4096, 4096], P(('ctx', 'exp')), may hold values from -70 to 70
- upstream: bfloat16 [4096, 4096], P(('ctx', 'exp')), may hold values from -6 to 6
- norm_gain: float32 [4096], replicated, may hold values from 0.5 to 1.5
- router: bfloat16 [4096, 8], replicated, may hold values from -4 to 4
- expert_ids: int32 [4096, 8], P(('ctx', 'exp')), may hold values from 0 to 7, as said below
- w_gate: bfloat16 [8, 4096, 1536], P('ctx', None, 'exp'), may hold values from -0.09375 to 0.09375
- w_up: bfloat16 [8, 4096, 1536], P('ctx', None, 'exp'), may hold values from -0.09375 to 0.09375
- w_down: bfloat16 [8, 1536, 4096], P('ctx', 'exp'), may hold values from -0.15625 to 0.15625
Outputs:
- grad_input: bfloat16 [4096, 4096], P(('ctx', 'exp'))
Inputs may be any that keep to these rules, and one draw needn't show every extreme that they name: `expert_ids`: A token's 8 entries differ. Among the rows of one device, no expert is named in column 0 by more than 24 rows, and in every device's rows one expert is named there by exactly 24.
All inputs are finite; a program needn't handle non-finite values.
Results may differ from a plain program's by a relative error of at most 0.012.
Values may be sent and summed in bfloat16 or wider, within the bound.
A program may use at most 128 MiB of HBM per device.

v0:
```python
import jax
import jax.numpy as jnp
from jax import lax
from jax.sharding import PartitionSpec as P

EPSILON = 1e-06


def silu_parts(pre_value):
    sigmoid_value = jax.nn.sigmoid(pre_value)
    return (pre_value * sigmoid_value, sigmoid_value * (1.0 + pre_value * (1.0 - sigmoid_value)))


def dispatch(stacked, experts, capacity, model_width):
    layers = stacked.shape[0]
    shaped = stacked.reshape(layers, experts, capacity, model_width)
    moved = lax.all_to_all(shaped, "ctx", split_axis=1, concat_axis=1, tiled=True)
    grouped = lax.all_gather(moved, "exp", axis=1, tiled=True)
    return grouped.reshape(layers, -1, model_width)


def place(values, target, slot_total):
    empty = jnp.zeros((values.shape[0], slot_total, values.shape[2]), values.dtype)
    return empty.at[:, target, :].set(values)


def per_device(hidden_states, upstream, norm_gain, router, expert_ids, w_gate, w_up, w_down):
    tok_rows, model_width = hidden_states.shape
    experts = router.shape[1]
    capacity = 3 * tok_rows // (2 * experts)
    slot_total = experts * capacity
    widened = hidden_states.astype(jnp.float32)
    inverse = lax.rsqrt(jnp.mean(widened * widened, axis=1, keepdims=True) + EPSILON)
    normed = (widened * inverse * norm_gain).astype(jnp.bfloat16)
    logits = jnp.dot(normed, router, preferred_element_type=jnp.float32)
    probability = jax.nn.softmax(logits, axis=1)
    labels = jnp.arange(experts, dtype=jnp.int32)
    chosen = (expert_ids[:, :, None] == labels).astype(jnp.float32)
    primary = chosen[:, 0, :]
    member = jnp.sum(chosen, axis=1)
    top_prob = jnp.sum(probability * primary, axis=1)
    route_mass = jnp.sum(probability * member, axis=1)
    gate_value = top_prob / route_mass
    upstream_wide = upstream.astype(jnp.float32)
    scaled_grad = (gate_value[:, None] * upstream_wide).astype(jnp.bfloat16)
    before = jnp.cumsum(primary, axis=0) - primary
    slot_index = jnp.sum(before * primary, axis=1).astype(jnp.int32)
    target = expert_ids[:, 0] * capacity + slot_index
    expert_rows = dispatch(place(normed[None], target, slot_total), experts, capacity, model_width)[
        0
    ]
    gate_block = w_gate[0]
    up_block = w_up[0]
    down_block = w_down[0]
    pre_gate = jnp.dot(expert_rows, gate_block, preferred_element_type=jnp.float32)
    pre_up = jnp.dot(expert_rows, up_block, preferred_element_type=jnp.float32)
    activated, act_slope = silu_parts(pre_gate)
    hidden = (activated * pre_up).astype(jnp.bfloat16)
    summed = lax.psum_scatter(
        jnp.dot(hidden, down_block, preferred_element_type=jnp.float32).astype(jnp.bfloat16),
        "exp",
        scatter_dimension=0,
        tiled=True,
    )
    outgoing = summed.reshape(experts, capacity, model_width)
    returned = lax.all_to_all(outgoing, "ctx", split_axis=0, concat_axis=0, tiled=True).reshape(
        slot_total, model_width
    )
    expert_out = returned[target].astype(jnp.float32)
    grad_rows = dispatch(
        place(scaled_grad[None], target, slot_total), experts, capacity, model_width
    )[0]
    hidden_grad = lax.dot_general(
        grad_rows, down_block, (((1,), (1,)), ((), ())), preferred_element_type=jnp.float32
    )
    grad_pre_gate = (hidden_grad * pre_up * act_slope).astype(jnp.bfloat16)
    grad_pre_up = (hidden_grad * activated).astype(jnp.bfloat16)
    gate_part = lax.dot_general(
        grad_pre_gate, gate_block, (((1,), (1,)), ((), ())), preferred_element_type=jnp.float32
    )
    up_part = lax.dot_general(
        grad_pre_up, up_block, (((1,), (1,)), ((), ())), preferred_element_type=jnp.float32
    )
    grad_summed = lax.psum_scatter(
        (gate_part + up_part).astype(jnp.bfloat16), "exp", scatter_dimension=0, tiled=True
    )
    grad_outgoing = grad_summed.reshape(experts, capacity, model_width)
    grad_returned = lax.all_to_all(
        grad_outgoing, "ctx", split_axis=0, concat_axis=0, tiled=True
    ).reshape(slot_total, model_width)
    expert_grad = grad_returned[target].astype(jnp.float32)
    gate_grad = jnp.sum(upstream_wide * expert_out, axis=1)
    prob_grad = gate_grad[:, None] * (
        primary / route_mass[:, None] - (top_prob / (route_mass * route_mass))[:, None] * member
    )
    logit_grad = probability * (prob_grad - jnp.sum(probability * prob_grad, axis=1, keepdims=True))
    normed_grad = expert_grad + jnp.dot(
        logit_grad, router.astype(jnp.float32).T, precision=lax.Precision.HIGHEST
    )
    scaled = normed_grad * norm_gain
    grad_input = (
        inverse * scaled
        - widened * inverse**3 * jnp.sum(scaled * widened, axis=1, keepdims=True) / model_width
    )
    return grad_input.astype(jnp.bfloat16)


def solution(mesh):
    placed = (
        P(("ctx", "exp"), None),
        P(("ctx", "exp"), None),
        P(),
        P(),
        P(("ctx", "exp"), None),
        P("ctx", None, "exp"),
        P("ctx", None, "exp"),
        P("ctx", "exp", None),
    )
    return jax.shard_map(
        per_device, mesh=mesh, in_specs=placed, out_specs=P(("ctx", "exp"), None), check_vma=False
    )
```

profile of v0, /device:TPU:0, one launch (start us, length us, event | category | flops | bytes accessed | tf_op | source)
XLA Modules:
  0.0 332.9 jit_solution(14029999209317259293)
XLA Ops:
  8.2 1.5 fusion.13
  10.1 1.7 fusion.47
  12.6 4.2 %scatter_custom_fusion.1 = bf16[192,4096]{1,0:T(8,128)(2,1)} fusion(s32[128]{0:T(128)S(1)} %fusion.42, bf16[]{:T(256)} %constant.4.clone.1, bf16[128,4096]{1,0:T(8,128)(2,1)} %param.8, f32[4096]{0:T(1024)S(1)} %copy-done.12, f32[128]{0:T(128)S(1)} %get-tuple-element.11), kind=kCustom, calls=%fused_computation.41 | custom fusion | flops 2097152 | bytes 2638338 | tf_op jit(solution)/shard_map/scatter | solution.py:24
  16.7 44.4 %all_to_all.20 = bf16[1,8,24,4096]{3,2,0,1:T(8,128)(2,1)} all-to-all(bf16[1,8,24,4096]{3,2,0,1:T(8,128)(2,1)} %bitcast.54), channel_id=1, replica_groups=mesh['ctx'=8,'exp'=4] {'ctx'}, dimensions={1} | all-to-all | bytes 3145728 | tf_op jit(solution)/shard_map/all_to_all | solution.py:17
  61.2 4.1 %scatter_custom_fusion = bf16[192,4096]{1,0:T(8,128)(2,1)} fusion(s32[128]{0:T(128)S(1)} %fusion.42, bf16[128,4096]{1,0:T(8,128)(2,1)} %param.9, f32[128]{0:T(128)S(1)} %get-tuple-element.9, bf16[]{:T(256)} %constant.4.clone.1), kind=kCustom, calls=%fused_computation.39 | custom fusion | flops 1572864 | bytes 2621954 | tf_op jit(solution)/shard_map/scatter | solution.py:24
  65.3 40.5 %all_to_all.21 = bf16[1,8,24,4096]{3,2,0,1:T(8,128)(2,1)} all-to-all(bf16[1,8,24,4096]{3,2,0,1:T(8,128)(2,1)} %bitcast.53), channel_id=1, replica_groups=mesh['ctx'=8,'exp'=4] {'ctx'}, dimensions={1} | all-to-all | bytes 3145728 | tf_op jit(solution)/shard_map/all_to_all | solution.py:17
  106.7 6.6 %fusion.3 = f32[768,384]{1,0:T(8,128)S(1)} fusion(bf16[768,4096]{1,0:T(8,128)(2,1)} %bitcast.57, bf16[1,4096,384]{2,1,0:T(8,128)(2,1)} %param.13), kind=kOutput, calls=%fused_computation.14 | convolution fusion | flops 2415919104 | bytes 10616832 | tf_op jit(solution)/shard_map/dot_general | solution.py:55
  113.3 3.4 %fusion.6 = f32[768,384]{1,0:T(8,128)S(1)} fusion(bf16[768,4096]{1,0:T(8,128)(2,1)S(1)} %bitcast.58, bf16[1,4096,384]{2,1,0:T(8,128)(2,1)S(1)} %copy-done.8), kind=kOutput, calls=%fused_computation.17 | convolution fusion | flops 2415919104 | bytes 10616832 | tf_op jit(solution)/shard_map/dot_general | solution.py:56
  117.7 5.3 %convolution_convert_fusion = bf16[768,4096]{1,0:T(8,128)(2,1)} fusion(bf16[1,384,4096]{2,1,0:T(8,128)(2,1)S(1)} %copy-done, f32[768,384]{1,0:T(8,128)S(1)} %fusion.6, f32[768,384]{1,0:T(8,128)S(1)} %fusion.3), kind=kOutput, calls=%fused_computation.5 | convolution fusion | flops 2420834304 | bytes 11796480 | tf_op jit(solution)/shard_map/dot_general | solution.py:60
  123.3 31.4 %all-gather.3.cloned.1.call-done = bf16[1,32,24,4096]{3,2,0,1:T(8,128)(2,1)} async-done(((bf16[1,8,24,4096]{3,2,0,1:T(8,128)(2,1)}), bf16[1,32,24,4096]{3,2,0,1:T(8,128)(2,1)}) %all-gather.3.cloned.1.call-update) | async-done | bytes 6291472 | tf_op jit(solution)/shard_map/all_gather | solution.py:18
  154.7 5.7 %fusion.9 = f32[768,384]{1,0:T(8,128)S(1)} fusion(bf16[768,4096]{1,0:T(8,128)(2,1)} %bitcast.59, bf16[1,384,4096]{2,1,0:T(8,128)(2,1)S(1)} %copy-done), kind=kOutput, calls=%fused_computation.20 | convolution fusion | flops 2415919104 | bytes 10616832 | tf_op jit(solution)/shard_map/dot_general | solution.py:73
  160.4 1.0 copy-done.6
  161.4 3.6 %fusion.1 = f32[768,4096]{1,0:T(8,128)S(1)} fusion(bf16[1,4096,384]{2,1,0:T(8,128)(2,1)S(1)} %copy-done.7, f32[768,384]{1,0:T(8,128)S(1)} %copy-done.5, f32[768,384]{1,0:T(8,128)S(1)} %fusion.9, f32[768,384]{1,0:T(8,128)S(1)} %copy-done.10), kind=kOutput, calls=%fused_computation.12 | convolution fusion | flops 2418868224 | bytes 19267584 | tf_op jit(solution)/shard_map/dot_general | solution.py:78
  164.9 10.1 %add_convert_fusion = bf16[768,4096]{1,0:T(8,128)(2,1)} fusion(f32[768,4096]{1,0:T(8,128)S(1)} %fusion.1, bf16[1,4096,384]{2,1,0:T(8,128)(2,1)} %param.14, f32[768,384]{1,0:T(8,128)} %copy-done.6, f32[768,384]{1,0:T(8,128)} %copy-done.4), kind=kOutput, calls=%fused_computation.4 | convolution fusion | flops 2423980032 | bytes 24379392 | tf_op jit(solution)/shard_map/dot_general | solution.py:81
  175.1 40.5 %reduce-scatter.5.cloned.1.call-done = bf16[192,4096]{1,0:T(8,128)(2,1)} async-done(((bf16[768,4096]{1,0:T(8,128)(2,1)}), bf16[192,4096]{1,0:T(8,128)(2,1)}) %reduce-scatter.5.cloned.1.call-update) | async-done | bytes 1572880 | tf_op jit(solution)/shard_map/reduce_scatter | solution.py:59
  215.6 5.5 %all-to-all-start.3 = ((bf16[8,24,4096]{2,1,0:T(8,128)(2,1)}), bf16[8,24,4096]{2,1,0:T(8,128)(2,1)S(1)}, u32[]{:S(2)}, u32[]{:S(2)}) async-start(bf16[8,24,4096]{2,1,0:T(8,128)(2,1)} %bitcast.55), calls=%async_computation.5 | async-start | bytes 3145728 | tf_op jit(solution)/shard_map/all_to_all | solution.py:66
  221.1 55.4 %reduce-scatter.3.cloned.1.call-done = bf16[192,4096]{1,0:T(8,128)(2,1)} async-done(((bf16[768,4096]{1,0:T(8,128)(2,1)}), bf16[192,4096]{1,0:T(8,128)(2,1)}) %reduce-scatter.3.cloned.1.call-update) | async-done | bytes 1572880 | tf_op jit(solution)/shard_map/reduce_scatter | solution.py:84
  276.5 5.5 %all-to-all-start.2 = ((bf16[8,24,4096]{2,1,0:T(8,128)(2,1)}), bf16[8,24,4096]{2,1,0:T(8,128)(2,1)S(1)}, u32[]{:S(2)}, u32[]{:S(2)}) async-start(bf16[8,24,4096]{2,1,0:T(8,128)(2,1)} %bitcast.56), calls=%async_computation.3 | async-start | bytes 3145728 | tf_op jit(solution)/shard_map/all_to_all | solution.py:88
  282.1 2.2 gather_fusion.1
  284.2 1.9 fusion.12
  286.1 32.9 %all-to-all-done.2 = bf16[8,24,4096]{2,1,0:T(8,128)(2,1)S(1)} async-done(((bf16[8,24,4096]{2,1,0:T(8,128)(2,1)}), bf16[8,24,4096]{2,1,0:T(8,128)(2,1)S(1)}, u32[]{:S(2)}, u32[]{:S(2)}) %all-to-all-start.2) | async-done | bytes 1572896 | tf_op jit(solution)/shard_map/all_to_all | solution.py:88
  319.1 2.2 gather_fusion
  321.3 2.8 fusion.20
  324.1 1.6 fusion.19
  (50 shorter events, 5.8 us)
Async XLA Ops:
  6.5 111.2 %copy-start = (bf16[1,384,4096]{2,1,0:T(8,128)(2,1)S(1)}, bf16[1,384,4096]{2,1,0:T(8,128)(2,1)}, u32[]{:S(2)}) copy-start(bf16[1,384,4096]{2,1,0:T(8,128)(2,1)} %param.15) | copy-start | bytes 9437188
  6.5 6.0 %copy-start.12 = (f32[4096]{0:T(1024)S(1)}, f32[4096]{0:T(1024)}, u32[]{:S(2)}) copy-start(f32[4096]{0:T(1024)} %param.10) | copy-start | bytes 49156
  6.5 100.1 %all-gather.5.cloned.1.call-start = ((), (), s32[]{:S(2)}) async-start(), calls=%async_computation.7 | async-start | bytes 7864320 | tf_op jit(solution)/shard_map/all_gather | solution.py:18
  61.1 93.6 %all-gather.3.cloned.1.call-start = ((), (), s32[]{:S(2)}) async-start(), calls=%async_computation.6 | async-start | bytes 7864320 | tf_op jit(solution)/shard_map/all_gather | solution.py:18
  105.8 109.8 %reduce-scatter.5.cloned.1.call-start = ((), (), s32[]{:S(2)}) async-start(), calls=%async_computation.9 | async-start | bytes 7864320 | tf_op jit(solution)/shard_map/reduce_scatter | solution.py:59
  106.7 6.6 %copy-start.8 = (bf16[1,4096,384]{2,1,0:T(8,128)(2,1)S(1)}, bf16[1,4096,384]{2,1,0:T(8,128)(2,1)}, u32[]{:S(2)}) copy-start(bf16[1,4096,384]{2,1,0:T(8,128)(2,1)} %param.14) | copy-start | bytes 9437188
  106.7 6.6 %copy-start.13 = (bf16[1,32,24,4096]{3,2,0,1:T(8,128)(2,1)S(1)}, bf16[1,32,24,4096]{3,2,0,1:T(8,128)(2,1)}, u32[]{:S(2)}) copy-start(bf16[1,32,24,4096]{3,2,0,1:T(8,128)(2,1)} %all-gather.5.cloned.1.call-done) | copy-start | bytes 18874372
  113.3 3.4 %copy-start.4 = (f32[768,384]{1,0:T(8,128)}, f32[768,384]{1,0:T(8,128)S(1)}, u32[]{:S(2)}) copy-start(f32[768,384]{1,0:T(8,128)S(1)} %fusion.3) | copy-start | bytes 3538948
  116.7 1.0 copy-start.9
  123.1 153.5 %reduce-scatter.3.cloned.1.call-start = ((), (), s32[]{:S(2)}) async-start(), calls=%async_computation.8 | async-start | bytes 7864320 | tf_op jit(solution)/shard_map/reduce_scatter | solution.py:84
  154.7 6.7 %copy-start.5 = (f32[768,384]{1,0:T(8,128)S(1)}, f32[768,384]{1,0:T(8,128)}, u32[]{:S(2)}) copy-start(f32[768,384]{1,0:T(8,128)} %copy-done.4) | copy-start | bytes 3538948
  154.7 6.7 %copy-start.7 = (bf16[1,4096,384]{2,1,0:T(8,128)(2,1)S(1)}, bf16[1,4096,384]{2,1,0:T(8,128)(2,1)}, u32[]{:S(2)}) copy-start(bf16[1,4096,384]{2,1,0:T(8,128)(2,1)} %param.13) | copy-start | bytes 9437188
  154.7 6.7 %copy-start.10 = (f32[768,384]{1,0:T(8,128)S(1)}, f32[768,384]{1,0:T(8,128)}, u32[]{:S(2)}) copy-start(f32[768,384]{1,0:T(8,128)} %copy-done.9) | copy-start | bytes 3538948
  160.3 1.0 copy-start.6
  215.6 60.9 %all-to-all-start.3 = ((bf16[8,24,4096]{2,1,0:T(8,128)(2,1)}), bf16[8,24,4096]{2,1,0:T(8,128)(2,1)S(1)}, u32[]{:S(2)}, u32[]{:S(2)}) async-start(bf16[8,24,4096]{2,1,0:T(8,128)(2,1)} %bitcast.55), calls=%async_computation.5 | async-start | bytes 3145728 | tf_op jit(solution)/shard_map/all_to_all | solution.py:66
  276.5 42.5 %all-to-all-start.2 = ((bf16[8,24,4096]{2,1,0:T(8,128)(2,1)}), bf16[8,24,4096]{2,1,0:T(8,128)(2,1)S(1)}, u32[]{:S(2)}, u32[]{:S(2)}) async-start(bf16[8,24,4096]{2,1,0:T(8,128)(2,1)} %bitcast.56), calls=%async_computation.3 | async-start | bytes 3145728 | tf_op jit(solution)/shard_map/all_to_all | solution.py:88
  319.1 2.2 copy-start.2
  319.1 2.2 copy-start.11
  321.3 2.8 copy-start.3
  324.1 2.3 copy-start.1
Sparse Core Ops, SparseCore 0:
  61.2 45.4 all-gather.4
  108.2 46.3 all-gather.2
  157.2 58.3 reduce-scatter.4
  218.2 58.3 reduce-scatter.2
where the time goes:
time: 333 us
  waiting for transfers between devices  161 us (48%)
  blocking collectives  84.9 us (25%)
  matrix products  39.1 us (12%)
  other arithmetic  15.9 us (5%)
  between operations  13.3 us (4%)
  starting transfers between devices  11.3 us (3%)
  local copies, waits for them, and re-layouts  7.26 us (2%)
    all_to_all x2, blocking collectives, dispatch(): lax.all_to_all(shaped, 'ctx', split_axis=1, concat_axis=1, tiled=True)  84.9 us
    reduce_scatter x1, waiting for transfers between devices, per_device(): lax.psum_scatter((gate_part + up_part).astype(jnp.bfloat16), 'exp', scatt...  55.4 us
    reduce_scatter x1, waiting for transfers between devices, per_device(): lax.psum_scatter(jnp.dot(hidden, down_block, preferred_element_type=jnp.f...  40.5 us
    all_to_all x1, waiting for transfers between devices, per_device(): lax.all_to_all(grad_outgoing, 'ctx', split_axis=0, concat_axis=0, tiled=T...  32.9 us
    all_gather x2, waiting for transfers between devices, dispatch(): grouped = lax.all_gather(moved, 'exp', axis=1, tiled=True)  32.2 us
    dot_general x1, matrix products, per_device(): lax.dot_general(grad_pre_up, up_block, (((1,), (1,)), ((), ())), preferre...  10.1 us
    scatter x2, other arithmetic, place(): return empty.at[:, target, :].set(values)  8.26 us
  transfers between devices with their start and end apart: 6, of which 5 were waited for; matrix products, arithmetic and copies ran while one was open for 13% of the time, Pallas kernels for 0%

commit v1 on v0

--- a/solution.py
+++ b/solution.py
@@ -15,7 +15,14 @@
     layers = stacked.shape[0]
     shaped = stacked.reshape(layers, experts, capacity, model_width)
     moved = lax.all_to_all(shaped, "ctx", split_axis=1, concat_axis=1, tiled=True)
-    grouped = lax.all_gather(moved, "exp", axis=1, tiled=True)
+    ways = lax.axis_size("exp")
+    pieces = [moved]
+    for far in range(1, ways):
+        pieces.append(
+            lax.ppermute(pieces[far - 1], "exp", [(d, (d - 1) % ways) for d in range(ways)])
+        )
+    line = jnp.concatenate(pieces, axis=1)
+    grouped = jnp.roll(line, lax.axis_index("exp") * moved.shape[1], axis=1)
     return grouped.reshape(layers, -1, model_width)
 
 

time: 333 us -> 400 us (1.20)
  waiting for transfers between devices: 161 us -> 274 us
  blocking collectives: 84.9 us -> 0 us
  other arithmetic: 15.9 us -> 35.2 us
  starting transfers between devices: 11.3 us -> 30.5 us
    all_to_all x2 -> x0, blocking collectives: 84.9 us -> none  [dispatch(): lax.all_to_all(shaped, 'ctx', split_axis=1, concat_axis=1, tiled=True)]
    ppermute x0 -> x6, waiting for transfers between devices: none -> 77.1 us  [dispatch(): lax.ppermute(pieces[far - 1], 'exp', [(d, (d - 1) % ways) for d in range(...]
    all_to_all x0 -> x2, waiting for transfers between devices: none -> 69.3 us  [dispatch(): lax.all_to_all(shaped, 'ctx', split_axis=1, concat_axis=1, tiled=True)]
    all_gather x2 -> x0, waiting for transfers between devices: 32.2 us -> none  [dispatch(): grouped = lax.all_gather(moved, 'exp', axis=1, tiled=True)]
    concatenate x0 -> x1, other arithmetic: none -> 19.3 us  [dispatch(): grouped = jnp.roll(line, lax.axis_index('exp') * moved.shape[1], axis=1)]
    all_to_all x0 -> x2, starting transfers between devices: none -> 11.5 us  [dispatch(): lax.all_to_all(shaped, 'ctx', split_axis=1, concat_axis=1, tiled=True)]
    ppermute x0 -> x6, starting transfers between devices: none -> 7.6 us  [dispatch(): lax.ppermute(pieces[far - 1], 'exp', [(d, (d - 1) % ways) for d in range(...]
  transfers between devices with their start and end apart: 6 -> 12, of which waited for: 5 -> 10; matrix products, arithmetic and copies ran while one was open for 13% -> 7% of each run, Pallas kernels for 0% -> 0%
where the time goes in v1:
time: 400 us; the launch traced here: 399 us
  waiting for transfers between devices  274 us (68%)
  matrix products  37.4 us (9%)
  other arithmetic  35.2 us (9%)
  starting transfers between devices  30.5 us (8%)
  between operations  13.6 us (3%)
  local copies, waits for them, and re-layouts  8.47 us (2%)
    ppermute x6, waiting for transfers between devices, dispatch(): lax.ppermute(pieces[far - 1], 'exp', [(d, (d - 1) % ways) for d in range(...  77.1 us
    all_to_all x2, waiting for transfers between devices, dispatch(): lax.all_to_all(shaped, 'ctx', split_axis=1, concat_axis=1, tiled=True)  69.3 us
    reduce_scatter x1, waiting for transfers between devices, per_device(): lax.psum_scatter((gate_part + up_part).astype(jnp.bfloat16), 'exp', scatt...  55.6 us
    reduce_scatter x1, waiting for transfers between devices, per_device(): lax.psum_scatter(jnp.dot(hidden, down_block, preferred_element_type=jnp.f...  39.2 us
    all_to_all x1, waiting for transfers between devices, per_device(): lax.all_to_all(grad_outgoing, 'ctx', split_axis=0, concat_axis=0, tiled=T...  32.9 us
    concatenate x1, other arithmetic, dispatch(): grouped = jnp.roll(line, lax.axis_index('exp') * moved.shape[1], axis=1)  19.3 us
    all_to_all x2, starting transfers between devices, dispatch(): lax.all_to_all(shaped, 'ctx', split_axis=1, concat_axis=1, tiled=True)  11.5 us
    dot_general x1, matrix products, per_device(): lax.dot_general(grad_pre_up, up_block, (((1,), (1,)), ((), ())), preferre...  9.32 us
  transfers between devices with their start and end apart: 12, of which 10 were waited for; matrix products, arithmetic and copies ran while one was open for 7% of the time, Pallas kernels for 0%

profile of v1, /device:TPU:0, one launch (start us, length us, event | category | flops | bytes accessed | tf_op | source)
XLA Modules:
  0.0 399.3 jit_solution(2568159372863993069)
XLA Ops:
  12.6 4.2 %scatter_custom_fusion.1 = bf16[192,4096]{1,0:T(8,128)(2,1)} fusion(s32[128]{0:T(128)S(1)} %fusion.56, bf16[]{:T(256)} %constant.40.clone.1, bf16[128,4096]{1,0:T(8,128)(2,1)} %param.10, f32[4096]{0:T(1024)S(1)} %copy-done.13, f32[128]{0:T(128)S(1)} %get-tuple-element.12), kind=kCustom, calls=%fused_computation.71 | custom fusion | flops 2097152 | bytes 2638338 | tf_op jit(solution)/shard_map/scatter | solution.py:31
  16.7 7.3 %all-to-all-start.1 = ((bf16[1,8,24,4096]{3,2,0,1:T(8,128)(2,1)}), bf16[1,8,24,4096]{3,2,0,1:T(8,128)(2,1)}, u32[]{:S(2)}, u32[]{:S(2)}) async-start(bf16[1,8,24,4096]{3,2,0,1:T(8,128)(2,1)} %bitcast.52), calls=%async_computation.1 | async-start | bytes 3145728 | tf_op jit(solution)/shard_map/all_to_all | solution.py:17
  24.0 4.1 %scatter_custom_fusion = bf16[192,4096]{1,0:T(8,128)(2,1)} fusion(s32[128]{0:T(128)S(1)} %fusion.56, bf16[128,4096]{1,0:T(8,128)(2,1)} %param.11, f32[128]{0:T(128)S(1)} %get-tuple-element.10, bf16[]{:T(256)} %constant.40.clone.1), kind=kCustom, calls=%fused_computation.69 | custom fusion | flops 1572864 | bytes 2621954 | tf_op jit(solution)/shard_map/scatter | solution.py:31
  28.1 33.0 %all-to-all-done.1 = bf16[1,8,24,4096]{3,2,0,1:T(8,128)(2,1)} async-done(((bf16[1,8,24,4096]{3,2,0,1:T(8,128)(2,1)}), bf16[1,8,24,4096]{3,2,0,1:T(8,128)(2,1)}, u32[]{:S(2)}, u32[]{:S(2)}) %all-to-all-start.1) | async-done | bytes 1572896 | tf_op jit(solution)/shard_map/all_to_all | solution.py:17
  61.1 4.3 %all-to-all-start = ((bf16[1,8,24,4096]{3,2,0,1:T(8,128)(2,1)}), bf16[1,8,24,4096]{3,2,0,1:T(8,128)(2,1)}, u32[]{:S(2)}, u32[]{:S(2)}) async-start(bf16[1,8,24,4096]{3,2,0,1:T(8,128)(2,1)} %bitcast.51), calls=%async_computation | async-start | bytes 3145728 | tf_op jit(solution)/shard_map/all_to_all | solution.py:17
  65.7 36.3 %all-to-all-done = bf16[1,8,24,4096]{3,2,0,1:T(8,128)(2,1)} async-done(((bf16[1,8,24,4096]{3,2,0,1:T(8,128)(2,1)}), bf16[1,8,24,4096]{3,2,0,1:T(8,128)(2,1)}, u32[]{:S(2)}, u32[]{:S(2)}) %all-to-all-start) | async-done | bytes 1572896 | tf_op jit(solution)/shard_map/all_to_all | solution.py:17
  103.7 16.6 %collective-permute-done = bf16[1,8,24,4096]{3,2,0,1:T(8,128)(2,1)S(1)} collective-permute-done((bf16[1,8,24,4096]{3,2,0,1:T(8,128)(2,1)}, bf16[1,8,24,4096]{3,2,0,1:T(8,128)(2,1)S(1)}, u32[]{:S(2)}, u32[]{:S(2)}) %collective-permute-start) | collective-permute-done | bytes 1572896 | tf_op jit(solution)/shard_map/ppermute | solution.py:22
  123.3 13.9 %collective-permute-done.4 = bf16[1,8,24,4096]{3,2,0,1:T(8,128)(2,1)} collective-permute-done((bf16[1,8,24,4096]{3,2,0,1:T(8,128)(2,1)}, bf16[1,8,24,4096]{3,2,0,1:T(8,128)(2,1)}, u32[]{:S(2)}, u32[]{:S(2)}) %collective-permute-start.4) | collective-permute-done | bytes 1572896 | tf_op jit(solution)/shard_map/ppermute | solution.py:22
  139.0 14.8 %collective-permute-done.1 = bf16[1,8,24,4096]{3,2,0,1:T(8,128)(2,1)} collective-permute-done((bf16[1,8,24,4096]{3,2,0,1:T(8,128)(2,1)S(1)}, bf16[1,8,24,4096]{3,2,0,1:T(8,128)(2,1)}, u32[]{:S(2)}, u32[]{:S(2)}) %collective-permute-start.1) | collective-permute-done | bytes 1572896 | tf_op jit(solution)/shard_map/ppermute | solution.py:22
  155.9 14.9 %collective-permute-done.5 = bf16[1,8,24,4096]{3,2,0,1:T(8,128)(2,1)} collective-permute-done((bf16[1,8,24,4096]{3,2,0,1:T(8,128)(2,1)}, bf16[1,8,24,4096]{3,2,0,1:T(8,128)(2,1)}, u32[]{:S(2)}, u32[]{:S(2)}) %collective-permute-start.5) | collective-permute-done | bytes 1572896 | tf_op jit(solution)/shard_map/ppermute | solution.py:22
  170.8 16.9 %collective-permute-done.2 = bf16[1,8,24,4096]{3,2,0,1:T(8,128)(2,1)} collective-permute-done((bf16[1,8,24,4096]{3,2,0,1:T(8,128)(2,1)}, bf16[1,8,24,4096]{3,2,0,1:T(8,128)(2,1)}, u32[]{:S(2)}, u32[]{:S(2)}) %collective-permute-start.2) | collective-permute-done | bytes 1572896 | tf_op jit(solution)/shard_map/ppermute | solution.py:22
  187.7 19.3 %fusion.3 = (bf16[1,32,24,4096]{3,2,0,1:T(8,128)(2,1)S(1)}, bf16[1,32,24,4096]{3,2,0,1:T(8,128)(2,1)}) fusion(s32[]{:T(128)S(6)} %select_n.21, bf16[1,8,24,4096]{3,2,0,1:T(8,128)(2,1)} %all-to-all-done.1, bf16[1,8,24,4096]{3,2,0,1:T(8,128)(2,1)} %collective-permute-done.3, bf16[1,8,24,4096]{3,2,0,1:T(8,128)(2,1)} %collective-permute-done.4, ...), kind=kLoop, calls=%fused_computation.25 | loop fusion | flops 44040192 | bytes 25165828 | tf_op jit(solution)/shard_map/jit(_roll_dynamic)/concatenate | solution.py:25
  207.0 5.5 %fusion.20 = f32[768,384]{1,0:T(8,128)S(1)} fusion(bf16[768,4096]{1,0:T(8,128)(2,1)S(1)} %bitcast.54, bf16[1,4096,384]{2,1,0:T(8,128)(2,1)} %param.16), kind=kOutput, calls=%fused_computation.47 | convolution fusion | flops 2415919104 | bytes 10616832 | tf_op jit(solution)/shard_map/dot_general | solution.py:63
  212.5 3.4 fusion.17
  216.9 5.5 %convolution_convert_fusion = bf16[768,4096]{1,0:T(8,128)(2,1)} fusion(bf16[1,384,4096]{2,1,0:T(8,128)(2,1)S(1)} %copy-done, f32[768,384]{1,0:T(8,128)S(1)} %fusion.20, f32[768,384]{1,0:T(8,128)S(1)} %fusion.17), kind=kOutput, calls=%fused_computation.21 | convolution fusion | flops 2420834304 | bytes 11796480 | tf_op jit(solution)/shard_map/dot_general | solution.py:67
  222.7 5.7 %fusion.23 = f32[768,384]{1,0:T(8,128)S(1)} fusion(bf16[768,4096]{1,0:T(8,128)(2,1)} %bitcast.53, bf16[1,384,4096]{2,1,0:T(8,128)(2,1)S(1)} %copy-done), kind=kOutput, calls=%fused_computation.50 | convolution fusion | flops 2415919104 | bytes 10616832 | tf_op jit(solution)/shard_map/dot_general | solution.py:80
  229.5 3.6 fusion.15
  233.0 9.3 %add_convert_fusion = bf16[768,4096]{1,0:T(8,128)(2,1)} fusion(f32[768,4096]{1,0:T(8,128)S(1)} %fusion.15, bf16[1,4096,384]{2,1,0:T(8,128)(2,1)} %param.16, f32[768,384]{1,0:T(8,128)} %copy-done.6, f32[768,384]{1,0:T(8,128)} %copy-done.4), kind=kOutput, calls=%fused_computation.20 | convolution fusion | flops 2423980032 | bytes 24379392 | tf_op jit(solution)/shard_map/dot_general | solution.py:88
  242.4 39.2 %reduce-scatter.5.cloned.1.call-done = bf16[192,4096]{1,0:T(8,128)(2,1)} async-done(((bf16[768,4096]{1,0:T(8,128)(2,1)}), bf16[192,4096]{1,0:T(8,128)(2,1)}) %reduce-scatter.5.cloned.1.call-update) | async-done | bytes 1572880 | tf_op jit(solution)/shard_map/reduce_scatter | solution.py:66
  281.6 5.5 %all-to-all-start.3 = ((bf16[8,24,4096]{2,1,0:T(8,128)(2,1)}), bf16[8,24,4096]{2,1,0:T(8,128)(2,1)S(1)}, u32[]{:S(2)}, u32[]{:S(2)}) async-start(bf16[8,24,4096]{2,1,0:T(8,128)(2,1)} %bitcast.56), calls=%async_computation.5 | async-start | bytes 3145728 | tf_op jit(solution)/shard_map/all_to_all | solution.py:73
  287.1 55.6 %reduce-scatter.3.cloned.1.call-done = bf16[192,4096]{1,0:T(8,128)(2,1)} async-done(((bf16[768,4096]{1,0:T(8,128)(2,1)}), bf16[192,4096]{1,0:T(8,128)(2,1)}) %reduce-scatter.3.cloned.1.call-update) | async-done | bytes 1572880 | tf_op jit(solution)/shard_map/reduce_scatter | solution.py:91
  342.7 5.5 %all-to-all-start.2 = ((bf16[8,24,4096]{2,1,0:T(8,128)(2,1)}), bf16[8,24,4096]{2,1,0:T(8,128)(2,1)S(1)}, u32[]{:S(2)}, u32[]{:S(2)}) async-start(bf16[8,24,4096]{2,1,0:T(8,128)(2,1)} %bitcast.57), calls=%async_computation.3 | async-start | bytes 3145728 | tf_op jit(solution)/shard_map/all_to_all | solution.py:95
  352.3 32.9 %all-to-all-done.2 = bf16[8,24,4096]{2,1,0:T(8,128)(2,1)S(1)} async-done(((bf16[8,24,4096]{2,1,0:T(8,128)(2,1)}), bf16[8,24,4096]{2,1,0:T(8,128)(2,1)S(1)}, u32[]{:S(2)}, u32[]{:S(2)}) %all-to-all-start.2) | async-done | bytes 1572896 | tf_op jit(solution)/shard_map/all_to_all | solution.py:95
  387.4 2.8 fusion.34
  (59 shorter events, 25.8 us)
Async XLA Ops:
  6.5 210.4 %copy-start = (bf16[1,384,4096]{2,1,0:T(8,128)(2,1)S(1)}, bf16[1,384,4096]{2,1,0:T(8,128)(2,1)}, u32[]{:S(2)}) copy-start(bf16[1,384,4096]{2,1,0:T(8,128)(2,1)} %param.17) | copy-start | bytes 9437188
  6.5 6.0 %copy-start.13 = (f32[4096]{0:T(1024)S(1)}, f32[4096]{0:T(1024)}, u32[]{:S(2)}) copy-start(f32[4096]{0:T(1024)} %param.12) | copy-start | bytes 49156
  16.7 44.4 %all-to-all-start.1 = ((bf16[1,8,24,4096]{3,2,0,1:T(8,128)(2,1)}), bf16[1,8,24,4096]{3,2,0,1:T(8,128)(2,1)}, u32[]{:S(2)}, u32[]{:S(2)}) async-start(bf16[1,8,24,4096]{3,2,0,1:T(8,128)(2,1)} %bitcast.52), calls=%async_computation.1 | async-start | bytes 3145728 | tf_op jit(solution)/shard_map/all_to_all | solution.py:17
  61.1 40.9 %all-to-all-start = ((bf16[1,8,24,4096]{3,2,0,1:T(8,128)(2,1)}), bf16[1,8,24,4096]{3,2,0,1:T(8,128)(2,1)}, u32[]{:S(2)}, u32[]{:S(2)}) async-start(bf16[1,8,24,4096]{3,2,0,1:T(8,128)(2,1)} %bitcast.51), calls=%async_computation | async-start | bytes 3145728 | tf_op jit(solution)/shard_map/all_to_all | solution.py:17
  65.4 216.2 %reduce-scatter.5.cloned.1.call-start = ((), (), s32[]{:S(2)}) async-start(), calls=%async_computation.7 | async-start | bytes 7864320 | tf_op jit(solution)/shard_map/reduce_scatter | solution.py:66
  65.4 36.6 %collective-permute-start.3 = (bf16[1,8,24,4096]{3,2,0,1:T(8,128)(2,1)}, bf16[1,8,24,4096]{3,2,0,1:T(8,128)(2,1)}, u32[]{:S(2)}, u32[]{:S(2)}) collective-permute-start(bf16[1,8,24,4096]{3,2,0,1:T(8,128)(2,1)} %all-to-all-done.1), channel_id=1, source_target_pairs={{0,3},{1,0},{2,1},{3,2},{4,7},{5,4},{6,5},{7,6},{8,11},{9,8},{10,9... | collective-permute-start | bytes 4718600 | tf_op jit(solution)/shard_map/ppermute | solution.py:22
  102.0 18.3 %collective-permute-start = (bf16[1,8,24,4096]{3,2,0,1:T(8,128)(2,1)}, bf16[1,8,24,4096]{3,2,0,1:T(8,128)(2,1)S(1)}, u32[]{:S(2)}, u32[]{:S(2)}) collective-permute-start(bf16[1,8,24,4096]{3,2,0,1:T(8,128)(2,1)} %all-to-all-done), channel_id=1, source_target_pairs={{0,3},{1,0},{2,1},{3,2},{4,7},{5,4},{6,5},{7,6},{8,11},{9,8},{10,9... | collective-permute-start | bytes 4718600 | tf_op jit(solution)/shard_map/ppermute | solution.py:22
  102.0 35.1 %collective-permute-start.4 = (bf16[1,8,24,4096]{3,2,0,1:T(8,128)(2,1)}, bf16[1,8,24,4096]{3,2,0,1:T(8,128)(2,1)}, u32[]{:S(2)}, u32[]{:S(2)}) collective-permute-start(bf16[1,8,24,4096]{3,2,0,1:T(8,128)(2,1)} %collective-permute-done.3), channel_id=1, source_target_pairs={{0,3},{1,0},{2,1},{3,2},{4,7},{5,4},{6,5},{7,6},{8,11},{9,8},{10,9... | collective-permute-start | bytes 4718600 | tf_op jit(solution)/shard_map/ppermute | solution.py:22
  120.3 1.2 copy-start.9
  121.5 32.4 %collective-permute-start.1 = (bf16[1,8,24,4096]{3,2,0,1:T(8,128)(2,1)S(1)}, bf16[1,8,24,4096]{3,2,0,1:T(8,128)(2,1)}, u32[]{:S(2)}, u32[]{:S(2)}) collective-permute-start(bf16[1,8,24,4096]{3,2,0,1:T(8,128)(2,1)S(1)} %collective-permute-done), channel_id=1, source_target_pairs={{0,3},{1,0},{2,1},{3,2},{4,7},{5,4},{6,5},{7,6},{8,11},{9,8},{10,9... | collective-permute-start | bytes 4718600 | tf_op jit(solution)/shard_map/ppermute | solution.py:22
  137.1 33.7 %collective-permute-start.5 = (bf16[1,8,24,4096]{3,2,0,1:T(8,128)(2,1)}, bf16[1,8,24,4096]{3,2,0,1:T(8,128)(2,1)}, u32[]{:S(2)}, u32[]{:S(2)}) collective-permute-start(bf16[1,8,24,4096]{3,2,0,1:T(8,128)(2,1)} %collective-permute-done.4), channel_id=1, source_target_pairs={{0,3},{1,0},{2,1},{3,2},{4,7},{5,4},{6,5},{7,6},{8,11},{9,8},{10,9... | collective-permute-start | bytes 4718600 | tf_op jit(solution)/shard_map/ppermute | solution.py:22
  153.9 33.8 %collective-permute-start.2 = (bf16[1,8,24,4096]{3,2,0,1:T(8,128)(2,1)}, bf16[1,8,24,4096]{3,2,0,1:T(8,128)(2,1)}, u32[]{:S(2)}, u32[]{:S(2)}) collective-permute-start(bf16[1,8,24,4096]{3,2,0,1:T(8,128)(2,1)} %collective-permute-done.1), channel_id=1, source_target_pairs={{0,3},{1,0},{2,1},{3,2},{4,7},{5,4},{6,5},{7,6},{8,11},{9,8},{10,9... | collective-permute-start | bytes 4718600 | tf_op jit(solution)/shard_map/ppermute | solution.py:22
  207.0 5.5 %copy-start.7 = (bf16[1,4096,384]{2,1,0:T(8,128)(2,1)S(1)}, bf16[1,4096,384]{2,1,0:T(8,128)(2,1)}, u32[]{:S(2)}) copy-start(bf16[1,4096,384]{2,1,0:T(8,128)(2,1)} %param.15) | copy-start | bytes 9437188
  212.5 3.4 copy-start.10
  222.4 120.3 %reduce-scatter.3.cloned.1.call-start = ((), (), s32[]{:S(2)}) async-start(), calls=%async_computation.6 | async-start | bytes 7864320 | tf_op jit(solution)/shard_map/reduce_scatter | solution.py:91
  222.7 6.8 %copy-start.5 = (f32[768,384]{1,0:T(8,128)S(1)}, f32[768,384]{1,0:T(8,128)}, u32[]{:S(2)}) copy-start(f32[768,384]{1,0:T(8,128)} %copy-done.4) | copy-start | bytes 3538948
  222.7 6.8 %copy-start.8 = (bf16[1,4096,384]{2,1,0:T(8,128)(2,1)S(1)}, bf16[1,4096,384]{2,1,0:T(8,128)(2,1)}, u32[]{:S(2)}) copy-start(bf16[1,4096,384]{2,1,0:T(8,128)(2,1)} %param.15) | copy-start | bytes 9437188
  222.7 6.7 %copy-start.11 = (f32[768,384]{1,0:T(8,128)S(1)}, f32[768,384]{1,0:T(8,128)}, u32[]{:S(2)}) copy-start(f32[768,384]{1,0:T(8,128)} %copy-done.10) | copy-start | bytes 3538948
  281.6 61.1 %all-to-all-start.3 = ((bf16[8,24,4096]{2,1,0:T(8,128)(2,1)}), bf16[8,24,4096]{2,1,0:T(8,128)(2,1)S(1)}, u32[]{:S(2)}, u32[]{:S(2)}) async-start(bf16[8,24,4096]{2,1,0:T(8,128)(2,1)} %bitcast.56), calls=%async_computation.5 | async-start | bytes 3145728 | tf_op jit(solution)/shard_map/all_to_all | solution.py:73
  342.7 42.5 %all-to-all-start.2 = ((bf16[8,24,4096]{2,1,0:T(8,128)(2,1)}), bf16[8,24,4096]{2,1,0:T(8,128)(2,1)S(1)}, u32[]{:S(2)}, u32[]{:S(2)}) async-start(bf16[8,24,4096]{2,1,0:T(8,128)(2,1)} %bitcast.57), calls=%async_computation.3 | async-start | bytes 3145728 | tf_op jit(solution)/shard_map/all_to_all | solution.py:95
  385.2 2.2 copy-start.2
  385.2 2.2 copy-start.12
  387.4 2.8 copy-start.3
  390.2 2.3 copy-start.1
  (2 other events, 2.1 us)
Sparse Core Ops, SparseCore 0:
  222.5 58.9 reduce-scatter.4
  284.3 58.3 reduce-scatter.2
